TPU v7x, 32 devices: a whole 2x2x4 slice. The times are simulated.
32 devices in a mesh: ctx: 8 (over z, y), tp: 4 (over x, core).
Axes of the slice: x: 2, y: 2, z: 4, core: 2. Of those that a mesh axis runs over, the one named last changes fastest.
Arguments:
- queries: bfloat16 [1024, 4096], P('ctx', 'tp'), may hold values from -64 to 64
- encoded_key_rows: bfloat16 [1024, 2048], P('ctx', 'tp'), may hold values from -6 to 6
- value_matrix_rows: bfloat16 [1024, 2048], P('ctx', 'tp'), may hold values from -6 to 6
- out_weight: bfloat16 [4096, 5376], P('tp'), may hold values from -0.5 to 0.5
- cotangent: bfloat16 [1024, 5376], P(('ctx', 'tp')), may hold values from -1.5 to 1.5
- doc_lengths: int32 [16], replicated, may hold values from 1 to 256, 1024 in all
Outputs:
- layer_out: bfloat16 [1024, 5376], P(('ctx', 'tp'))
- query_grad: bfloat16 [1024, 4096], P('ctx', 'tp')
- key_grad: bfloat16 [1024, 2048], P('ctx', 'tp')
- value_grad: bfloat16 [1024, 2048], P('ctx', 'tp')
Inputs may be any that keep to these rules, and one draw needn't show every extreme that they name: `doc_lengths`: they sum to 1024, and the longest document has exactly 256 tokens.
All inputs are finite; a program needn't handle non-finite values.
Results may differ from a plain program's by a relative error of at most 0.017.
Values may be sent and summed in bfloat16 or wider, within the bound.
No kernel may reach another device: no remote copies, remote signals or barrier semaphores. Data moves between devices by JAX's collectives and lax.ppermute only.
A program may use at most 64 MiB of HBM per device.

v0:
```python
import jax
import jax.numpy as jnp
from jax import lax
from jax.sharding import PartitionSpec as P

D = 5376
QUERY_HEADS = 32
KEY_VALUE_HEADS = 16
HEAD_SIZE = 128
WINDOW_SPAN = 1024


def passed_along(value, axis, steps):
    count = lax.axis_size(axis)
    leading, last = (max(0, -steps), min(count, count - steps))
    return lax.ppermute(value, axis, [(source, source + steps) for source in range(leading, last)])


def doc_index(positions, doc_ends):
    return jnp.sum((positions[:, None] >= doc_ends[None, :]).astype(jnp.int32), axis=1)


def allowed_pairs(query_pos, key_pos, doc_lengths):
    doc_ends = jnp.cumsum(doc_lengths)
    same_doc = doc_index(query_pos, doc_ends)[:, None] == doc_index(key_pos, doc_ends)[None, :]
    distance = query_pos[:, None] - key_pos[None, :]
    return same_doc & (distance >= 0) & (distance < WINDOW_SPAN) & (key_pos[None, :] >= 0)


def softmax_rows(scores, allowed):
    masked = jnp.where(allowed[None, None], scores, -jnp.inf)
    peak = jnp.max(masked, axis=-1, keepdims=True)
    unnorm = jnp.exp(masked - peak)
    return unnorm / jnp.sum(unnorm, axis=-1, keepdims=True)


def local(queries, encoded_key_rows, value_matrix_rows, out_weight, cotangent, doc_lengths):
    tok_rows = queries.shape[0]
    kv_cols = encoded_key_rows.shape[1]
    heads_kv = kv_cols // HEAD_SIZE
    query_group_size = QUERY_HEADS // KEY_VALUE_HEADS
    reach_count = WINDOW_SPAN // tok_rows
    score_scale = (D / QUERY_HEADS) ** (-0.5)
    device = lax.axis_index("ctx")
    key_value = jnp.concatenate([encoded_key_rows, value_matrix_rows], axis=1)
    behind = [passed_along(key_value, "ctx", distance) for distance in range(reach_count, 0, -1)]
    gathered = jnp.concatenate(behind + [key_value], axis=0)
    key_count = gathered.shape[0]
    keys_all = gathered[:, :kv_cols].reshape(key_count, heads_kv, HEAD_SIZE)
    values_all = gathered[:, kv_cols:].reshape(key_count, heads_kv, HEAD_SIZE)
    query_pos = device * tok_rows + jnp.arange(tok_rows, dtype=jnp.int32)
    key_pos = (device - reach_count) * tok_rows + jnp.arange(key_count, dtype=jnp.int32)
    allowed = allowed_pairs(query_pos, key_pos, doc_lengths)
    query_four = queries.reshape(tok_rows, heads_kv, query_group_size, HEAD_SIZE)
    scores = (
        jnp.einsum("pkgd,nkd->kgpn", query_four, keys_all, preferred_element_type=jnp.float32)
        * score_scale
    )
    probs = softmax_rows(scores, allowed)
    probabilities_narrow = probs.astype(jnp.bfloat16)
    attended = (
        jnp.einsum(
            "kgpn,nkd->pkgd", probabilities_narrow, values_all, preferred_element_type=jnp.float32
        )
        .astype(jnp.bfloat16)
        .reshape(tok_rows, heads_kv * query_group_size * HEAD_SIZE)
    )
    layer_out = lax.psum_scatter(
        jnp.dot(attended, out_weight, preferred_element_type=jnp.float32).astype(jnp.bfloat16),
        "tp",
        scatter_dimension=0,
        tiled=True,
    )
    attended_output_grad = lax.dot_general(
        lax.all_gather(cotangent, "tp", axis=0, tiled=True),
        out_weight,
        (((1,), (1,)), ((), ())),
        preferred_element_type=jnp.float32,
    ).astype(jnp.bfloat16)
    grad_four = attended_output_grad.reshape(tok_rows, heads_kv, query_group_size, HEAD_SIZE)
    prob_grad = jnp.einsum(
        "pkgd,nkd->kgpn", grad_four, values_all, preferred_element_type=jnp.float32
    )
    row_delta = jnp.sum(probs * prob_grad, axis=-1, keepdims=True)
    score_gradient = (probs * (prob_grad - row_delta) * score_scale).astype(jnp.bfloat16)
    query_grad = (
        jnp.einsum("kgpn,nkd->pkgd", score_gradient, keys_all, preferred_element_type=jnp.float32)
        .astype(jnp.bfloat16)
        .reshape(tok_rows, queries.shape[1])
    )
    key_terms = jnp.einsum(
        "hofw,fhot->wht", score_gradient, query_four, preferred_element_type=jnp.float32
    ).reshape(key_count, kv_cols)
    value_terms = jnp.einsum(
        "hofw,fhot->wht", probabilities_narrow, grad_four, preferred_element_type=jnp.float32
    ).reshape(key_count, kv_cols)
    grads = jnp.concatenate([key_terms, value_terms], axis=1)
    own_grad = grads[reach_count * tok_rows :]
    for distance in range(1, reach_count + 1):
        gradient_block = grads[
            (reach_count - distance) * tok_rows : (reach_count - distance + 1) * tok_rows
        ]
        own_grad = own_grad + passed_along(
            gradient_block.astype(jnp.bfloat16), "ctx", -distance
        ).astype(gradient_block.dtype)
    key_grad = own_grad[:, :kv_cols].astype(jnp.bfloat16)
    value_grad = own_grad[:, kv_cols:].astype(jnp.bfloat16)
    return (layer_out, query_grad, key_grad, value_grad)


def solution(mesh):
    in_specs = (
        P("ctx", "tp"),
        P("ctx", "tp"),
        P("ctx", "tp"),
        P("tp", None),
        P(("ctx", "tp"), None),
        P(),
    )
    out_specs = (P(("ctx", "tp"), None), P("ctx", "tp"), P("ctx", "tp"), P("ctx", "tp"))
    return jax.shard_map(local, mesh=mesh, in_specs=in_specs, out_specs=out_specs, check_vma=False)
```

profile of v0, /device:TPU:11, one launch (start us, length us, event | category | flops | bytes accessed | tf_op | source)
XLA Modules:
  0.0 171.9 jit_solution(3062393975751230981)
XLA Ops:
  9.3 3.1 %collective-permute-start.7 = (bf16[128,1024]{0,1:T(8,128)(2,1)S(1)}, bf16[128,1024]{0,1:T(8,128)(2,1)S(1)}, u32[]{:S(2)}, u32[]{:S(2)}) collective-permute-start(bf16[128,1024]{0,1:T(8,128)(2,1)S(1)} %pad_maximum_fusion.1), channel_id=1, source_target_pairs={{0,4},{4,8},{8,12},{12,16},{16,20},{20,24},{24,28},{1,5},{5,9},{9,... | collective-permute-start | bytes 786440 | tf_op jit(solution)/shard_map/ppermute | solution.py:16
  12.5 3.2 %collective-permute-start.6 = (bf16[128,1024]{0,1:T(8,128)(2,1)S(1)}, bf16[128,1024]{0,1:T(8,128)(2,1)S(1)}, u32[]{:S(2)}, u32[]{:S(2)}) collective-permute-start(bf16[128,1024]{0,1:T(8,128)(2,1)S(1)} %pad_maximum_fusion.1), channel_id=1, source_target_pairs={{0,8},{4,12},{8,16},{12,20},{16,24},{20,28},{1,9},{5,13},{9,17},{1... | collective-permute-start | bytes 786440 | tf_op jit(solution)/shard_map/ppermute | solution.py:16
  18.9 1.9 %fusion.22 = pred[128,1152]{0,1:T(8,128)(4,1)} fusion(s32[1152]{0:T(1024)S(1)} %iota_add_fusion, s32[128]{0:T(128)S(1)} %iota_add_fusion.1, s32[128]{0:T(128)S(1)} %convert_reduce_fusion.1, s32[1152]{0:T(1024)S(1)} %convert_reduce_fusion, pred[1152]{0:T(1024)(128)(4,1)S(1)} %broadcast_compare_fusion), kind=kLoop, calls=%fused_computation.35 | loop fusion | flops 1032192 | bytes 158848 | tf_op jit(solution)/shard_map/and | solution.py:27
  22.0 2.6 %collective-permute-start.3 = (bf16[128,1024]{0,1:T(8,128)(2,1)S(1)}, bf16[128,1024]{0,1:T(8,128)(2,1)S(1)}, u32[]{:S(2)}, u32[]{:S(2)}) collective-permute-start(bf16[128,1024]{0,1:T(8,128)(2,1)S(1)} %pad_maximum_fusion.1), channel_id=1, source_target_pairs={{0,20},{4,24},{8,28},{1,21},{5,25},{9,29},{2,22},{6,26},{10,30},{3... | collective-permute-start | bytes 786440 | tf_op jit(solution)/shard_map/ppermute | solution.py:16
  27.8 22.1 %collective-permute-done.3 = bf16[128,1024]{0,1:T(8,128)(2,1)S(1)} collective-permute-done((bf16[128,1024]{0,1:T(8,128)(2,1)S(1)}, bf16[128,1024]{0,1:T(8,128)(2,1)S(1)}, u32[]{:S(2)}, u32[]{:S(2)}) %collective-permute-start.3) | collective-permute-done | bytes 262176 | tf_op jit(solution)/shard_map/ppermute | solution.py:16
  50.0 5.6 %collective-permute-done.4 = bf16[128,1024]{0,1:T(8,128)(2,1)S(1)} collective-permute-done((bf16[128,1024]{0,1:T(8,128)(2,1)S(1)}, bf16[128,1024]{0,1:T(8,128)(2,1)S(1)}, u32[]{:S(2)}, u32[]{:S(2)}) %collective-permute-start.4) | collective-permute-done | bytes 262176 | tf_op jit(solution)/shard_map/ppermute | solution.py:16
  55.6 5.6 %collective-permute-done.5 = bf16[128,1024]{0,1:T(8,128)(2,1)S(1)} collective-permute-done((bf16[128,1024]{0,1:T(8,128)(2,1)S(1)}, bf16[128,1024]{0,1:T(8,128)(2,1)S(1)}, u32[]{:S(2)}, u32[]{:S(2)}) %collective-permute-start.5) | collective-permute-done | bytes 262176 | tf_op jit(solution)/shard_map/ppermute | solution.py:16
  62.3 3.8 %exponential_reduce_fusion = (f32[4,2,128]{2,1,0:T(2,128)S(1)}, f32[4,2,128,1152]{2,3,1,0:T(8,128)}) fusion(pred[128,1152]{0,1:T(8,128)(4,1)S(1)} %copy-done.2, bf16[1152,4,128,1]{0,2,3,1:T(8,128)(2,1)S(1)} %bitcast.94, bf16[128,4,2,128]{0,3,2,1:T(8,128)(2,1)S(1)} %bitcast.101), kind=kOutput, calls=%fused_computation.17 | convolution fusion | flops 306709632 | bytes 6311936 | tf_op jit(solution)/shard_map/sub | solution.py:33
  66.1 2.3 %convolution_convert_fusion.1 = bf16[4,128,2,128]{3,1,2,0:T(8,128)(2,1)S(1)} fusion(bf16[1152,4,128,1]{0,2,3,1:T(8,128)(2,1)S(1)} %bitcast.90, f32[4,2,128]{2,1,0:T(2,128)S(1)} %get-tuple-element.28, pred[128,1152]{0,1:T(8,128)(4,1)S(1)} %copy-done.2, bf16[1152,4,128,1]{0,2,3,1:T(8,128)(2,1)S(1)} %bitcast.95, bf16[128,4,2,128]{0,3,2,1:T(8,128)(2,1)S(1)} %bitcast.102), kind=kOutput, calls=%fused_computation.26 | convolution fusion | flops 610011264 | bytes 3035136 | tf_op jit(solution)/shard_map/kgpn,nkd->pkgd/dot_general | solution.py:62
  68.4 6.9 %convolution_convert_fusion = bf16[128,5376]{1,0:T(8,128)(2,1)} fusion(bf16[128,1024]{0,1:T(8,128)(2,1)S(1)} %bitcast.100, bf16[1024,5376]{1,0:T(8,128)(2,1)} %param.9), kind=kOutput, calls=%fused_computation.2 | convolution fusion | flops 1409974272 | bytes 12648448 | tf_op jit(solution)/shard_map/dot_general | solution.py:69
  75.4 8.2 %convolution_convert_fusion.2 = bf16[128,1024]{1,0:T(8,128)(2,1)S(1)} fusion(bf16[128,5376]{1,0:T(8,128)(2,1)} %all-gather.2.cloned.1.call-done, bf16[1024,5376]{1,0:T(8,128)(2,1)} %param.9), kind=kOutput, calls=%fused_computation.27 | convolution fusion | flops 1409417216 | bytes 12648448 | tf_op jit(solution)/shard_map/dot_general | solution.py:74
  83.7 3.0 %fusion.42 = f32[4,1152,128,2]{2,1,3,0:T(8,128)} fusion(bf16[1152,4,128,1]{0,2,3,1:T(8,128)(2,1)S(1)} %bitcast.91, bf16[128,4,2,128]{0,3,2,1:T(8,128)(2,1)S(1)} %bitcast.98), kind=kOutput, calls=%fused_computation.70 | convolution fusion | flops 301989888 | bytes 6160384 | tf_op jit(solution)/shard_map/pkgd,nkd->kgpn/dot_general | solution.py:81
  86.7 9.9 %fusion.10 = f32[4,1152,128,1]{1,2,3,0:T(8,128)} fusion(bf16[128,4,2,128]{0,3,2,1:T(8,128)(2,1)S(1)} %bitcast.103, f32[4,1152,128,2]{2,1,3,0:T(8,128)} %fusion.42, f32[4,2,128,1152]{2,3,1,0:T(8,128)} %get-tuple-element.29, f32[4,2,128]{2,1,0:T(2,128)S(1)} %get-tuple-element.28), kind=kOutput, calls=%fused_computation.19 | convolution fusion | flops 310249600 | bytes 12062720 | tf_op jit(solution)/shard_map/hofw,fhot->wht/dot_general | solution.py:91
  96.6 2.0 %copy.54 = f32[1152,512]{1,0:T(8,128)S(1)} copy(f32[1152,512]{0,1:T(8,128)} %bitcast.93) | data formatting | bytes 4718592 | tf_op jit(solution)/shard_map/reshape | solution.py:93
  98.7 4.9 %fusion.17 = f32[4,128,1152,1]{2,1,3,0:T(8,128)} fusion(bf16[128,4,2,128]{0,3,2,1:T(8,128)(2,1)} %bitcast.99, f32[4,2,128]{2,1,0:T(2,128)S(1)} %get-tuple-element.28, pred[128,1152]{0,1:T(8,128)(4,1)} %fusion.22, bf16[1152,4,128,1]{0,2,3,1:T(8,128)(2,1)S(1)} %bitcast.96, bf16[128,4,2,128]{0,3,2,1:T(8,128)(2,1)} %bitcast.104), kind=kOutput, calls=%fused_computation.28 | convolution fusion | flops 609880192 | bytes 4214784 | tf_op jit(solution)/shard_map/hofw,fhot->wht/dot_general | solution.py:94
  103.5 3.1 %copy.55 = f32[1152,512]{1,0:T(8,128)} copy(f32[1152,512]{0,1:T(8,128)} %bitcast.92) | data formatting | bytes 4718592 | tf_op jit(solution)/shard_map/reshape | solution.py:96
  106.7 2.0 %fusion.6 = bf16[1152,1024]{1,0:T(8,128)(2,1)S(1)} fusion(f32[1152,512]{1,0:T(8,128)} %copy.55, f32[1152,512]{1,0:T(8,128)S(1)} %copy.54), kind=kLoop, calls=%fused_computation.11 | loop fusion | flops 4718592 | bytes 7077888 | tf_op jit(solution)/shard_map/convert.9
  117.1 2.1 %collective-permute-done.8 = bf16[128,1024]{1,0:T(8,128)(2,1)} collective-permute-done((bf16[128,1024]{1,0:T(8,128)(2,1)S(1)}, bf16[128,1024]{1,0:T(8,128)(2,1)}, u32[]{:S(2)}, u32[]{:S(2)}) %collective-permute-start.8) | collective-permute-done | bytes 262176 | tf_op jit(solution)/shard_map/ppermute | solution.py:16
  121.8 4.4 %collective-permute-start.9 = (bf16[128,1024]{1,0:T(8,128)(2,1)}, bf16[128,1024]{1,0:T(8,128)(2,1)}, u32[]{:S(2)}, u32[]{:S(2)}) collective-permute-start(bf16[128,1024]{1,0:T(8,128)(2,1)} %get-tuple-element.23), channel_id=1, source_target_pairs={{8,0},{12,4},{16,8},{20,12},{24,16},{28,20},{9,1},{13,5},{17,9},{2... | collective-permute-start | bytes 786440 | tf_op jit(solution)/shard_map/ppermute | solution.py:16
  126.2 9.3 %fusion.16 = bf16[4,128,2,128]{3,1,2,0:T(8,128)(2,1)} fusion(bf16[1152,4,128,1]{0,2,3,1:T(8,128)(2,1)S(1)} %bitcast.97, f32[4,1152,128,2]{2,1,3,0:T(8,128)} %fusion.42, f32[4,2,128,1152]{2,3,1,0:T(8,128)} %get-tuple-element.29, f32[4,2,128]{2,1,0:T(2,128)S(1)} %get-tuple-element.28), kind=kOutput, calls=%fused_computation.25 | convolution fusion | flops 310380672 | bytes 10883072 | tf_op jit(solution)/shard_map/kgpn,nkd->pkgd/dot_general | solution.py:87
  137.3 1.9 %collective-permute-done.11 = bf16[128,1024]{1,0:T(8,128)(2,1)} collective-permute-done((bf16[128,1024]{1,0:T(8,128)(2,1)}, bf16[128,1024]{1,0:T(8,128)(2,1)}, u32[]{:S(2)}, u32[]{:S(2)}) %collective-permute-start.11) | collective-permute-done | bytes 262176 | tf_op jit(solution)/shard_map/ppermute | solution.py:16
  139.2 18.4 %collective-permute-done.10 = bf16[128,1024]{1,0:T(8,128)(2,1)} collective-permute-done((bf16[128,1024]{1,0:T(8,128)(2,1)}, bf16[128,1024]{1,0:T(8,128)(2,1)}, u32[]{:S(2)}, u32[]{:S(2)}) %collective-permute-start.10) | collective-permute-done | bytes 262176 | tf_op jit(solution)/shard_map/ppermute | solution.py:16
  157.6 4.8 %collective-permute-done.9 = bf16[128,1024]{1,0:T(8,128)(2,1)} collective-permute-done((bf16[128,1024]{1,0:T(8,128)(2,1)}, bf16[128,1024]{1,0:T(8,128)(2,1)}, u32[]{:S(2)}, u32[]{:S(2)}) %collective-permute-start.9) | collective-permute-done | bytes 262176 | tf_op jit(solution)/shard_map/ppermute | solution.py:16
  162.4 2.0 %fusion.32 = bf16[128,1024]{1,0:T(8,128)(2,1)S(1)} fusion(bf16[128,1024]{1,0:T(8,128)(2,1)} %collective-permute-done.15, bf16[128,1024]{1,0:T(8,128)(2,1)} %collective-permute-done.14, bf16[128,1024]{1,0:T(8,128)(2,1)} %collective-permute-done.13, bf16[128,1024]{1,0:T(8,128)(2,1)} %collective-permute-done.12, bf16[128,1024]{1,0:T(8,128)(2,1)} %collective-permute-done.11, ...), kind=kLoop, calls=%fused_computation.45 | loop fusion | flops 2359296 | bytes 7077888 | tf_op jit(solution)/shard_map/convert.1
  (59 shorter events, 24.4 us)
Async XLA Ops:
  7.2 68.2 %all-gather.2.cloned.1.call-start = ((), (), s32[]{:S(2)}) async-start(), calls=%async_computation.2 | async-start | bytes 1720320 | tf_op jit(solution)/shard_map/all_gather | solution.py:75
  9.3 52.0 %collective-permute-start.7 = (bf16[128,1024]{0,1:T(8,128)(2,1)S(1)}, bf16[128,1024]{0,1:T(8,128)(2,1)S(1)}, u32[]{:S(2)}, u32[]{:S(2)}) collective-permute-start(bf16[128,1024]{0,1:T(8,128)(2,1)S(1)} %pad_maximum_fusion.1), channel_id=1, source_target_pairs={{0,4},{4,8},{8,12},{12,16},{16,20},{20,24},{24,28},{1,5},{5,9},{9,... | collective-permute-start | bytes 786440 | tf_op jit(solution)/shard_map/ppermute | solution.py:16
  12.5 48.7 %collective-permute-start.6 = (bf16[128,1024]{0,1:T(8,128)(2,1)S(1)}, bf16[128,1024]{0,1:T(8,128)(2,1)S(1)}, u32[]{:S(2)}, u32[]{:S(2)}) collective-permute-start(bf16[128,1024]{0,1:T(8,128)(2,1)S(1)} %pad_maximum_fusion.1), channel_id=1, source_target_pairs={{0,8},{4,12},{8,16},{12,20},{16,24},{20,28},{1,9},{5,13},{9,17},{1... | collective-permute-start | bytes 786440 | tf_op jit(solution)/shard_map/ppermute | solution.py:16
  15.7 10.7 %collective-permute-start.2 = (bf16[128,1024]{0,1:T(8,128)(2,1)S(1)}, bf16[128,1024]{0,1:T(8,128)(2,1)S(1)}, u32[]{:S(2)}, u32[]{:S(2)}) collective-permute-start(bf16[128,1024]{0,1:T(8,128)(2,1)S(1)} %pad_maximum_fusion.1), channel_id=1, source_target_pairs={{0,24},{4,28},{1,25},{5,29},{2,26},{6,30},{3,27},{7,31}} | collective-permute-start | bytes 786440 | tf_op jit(solution)/shard_map/ppermute | solution.py:16
  16.3 8.3 %collective-permute-start.1 = (bf16[128,1024]{0,1:T(8,128)(2,1)S(1)}, bf16[128,1024]{0,1:T(8,128)(2,1)S(1)}, u32[]{:S(2)}, u32[]{:S(2)}) collective-permute-start(bf16[128,1024]{0,1:T(8,128)(2,1)S(1)} %pad_maximum_fusion.1), channel_id=1, source_target_pairs={{0,28},{1,29},{2,30},{3,31}} | collective-permute-start | bytes 786440 | tf_op jit(solution)/shard_map/ppermute | solution.py:16
  17.0 4.9 %collective-permute-start = (bf16[128,1024]{0,1:T(8,128)(2,1)S(1)}, bf16[128,1024]{0,1:T(8,128)(2,1)S(1)}, u32[]{:S(2)}, u32[]{:S(2)}) collective-permute-start(bf16[128,1024]{0,1:T(8,128)(2,1)S(1)} %pad_maximum_fusion.1), channel_id=1, source_target_pairs={} | collective-permute-start | bytes 786440 | tf_op jit(solution)/shard_map/ppermute | solution.py:16
  17.7 147.4 %reduce-scatter.2.cloned.1.call-start = ((), (), s32[]{:S(2)}) async-start(), calls=%async_computation.1 | async-start | bytes 1720320 | tf_op jit(solution)/shard_map/reduce_scatter | solution.py:68
  22.0 64.7 %copy-start.1 = (bf16[128,1024]{0,1:T(8,128)(2,1)}, bf16[128,1024]{0,1:T(8,128)(2,1)S(1)}, u32[]{:S(2)}) copy-start(bf16[128,1024]{0,1:T(8,128)(2,1)S(1)} %copy.71) | copy-start | bytes 786436
  22.0 27.9 %collective-permute-start.3 = (bf16[128,1024]{0,1:T(8,128)(2,1)S(1)}, bf16[128,1024]{0,1:T(8,128)(2,1)S(1)}, u32[]{:S(2)}, u32[]{:S(2)}) collective-permute-start(bf16[128,1024]{0,1:T(8,128)(2,1)S(1)} %pad_maximum_fusion.1), channel_id=1, source_target_pairs={{0,20},{4,24},{8,28},{1,21},{5,25},{9,29},{2,22},{6,26},{10,30},{3... | collective-permute-start | bytes 786440 | tf_op jit(solution)/shard_map/ppermute | solution.py:16
  24.7 30.8 %collective-permute-start.4 = (bf16[128,1024]{0,1:T(8,128)(2,1)S(1)}, bf16[128,1024]{0,1:T(8,128)(2,1)S(1)}, u32[]{:S(2)}, u32[]{:S(2)}) collective-permute-start(bf16[128,1024]{0,1:T(8,128)(2,1)S(1)} %pad_maximum_fusion.1), channel_id=1, source_target_pairs={{0,16},{4,20},{8,24},{12,28},{1,17},{5,21},{9,25},{13,29},{2,18},{... | collective-permute-start | bytes 786440 | tf_op jit(solution)/shard_map/ppermute | solution.py:16
  26.4 34.8 %collective-permute-start.5 = (bf16[128,1024]{0,1:T(8,128)(2,1)S(1)}, bf16[128,1024]{0,1:T(8,128)(2,1)S(1)}, u32[]{:S(2)}, u32[]{:S(2)}) collective-permute-start(bf16[128,1024]{0,1:T(8,128)(2,1)S(1)} %pad_maximum_fusion.1), channel_id=1, source_target_pairs={{0,12},{4,16},{8,20},{12,24},{16,28},{1,13},{5,17},{9,21},{13,25},... | collective-permute-start | bytes 786440 | tf_op jit(solution)/shard_map/ppermute | solution.py:16
  61.4 0.9 copy-start.2
  83.7 3.0 %copy-start = (bf16[128,1024]{0,1:T(8,128)(2,1)}, bf16[128,1024]{0,1:T(8,128)(2,1)S(1)}, u32[]{:S(2)}) copy-start(bf16[128,1024]{0,1:T(8,128)(2,1)S(1)} %copy.72) | copy-start | bytes 786436
  109.8 9.4 %collective-permute-start.8 = (bf16[128,1024]{1,0:T(8,128)(2,1)S(1)}, bf16[128,1024]{1,0:T(8,128)(2,1)}, u32[]{:S(2)}, u32[]{:S(2)}) collective-permute-start(bf16[128,1024]{1,0:T(8,128)(2,1)S(1)} %get-tuple-element.16), channel_id=1, source_target_pairs={{4,0},{8,4},{12,8},{16,12},{20,16},{24,20},{28,24},{5,1},{9,5},{13... | collective-permute-start | bytes 786440 | tf_op jit(solution)/shard_map/ppermute | solution.py:16
  111.7 8.8 %collective-permute-start.15 = (bf16[128,1024]{1,0:T(8,128)(2,1)S(1)}, bf16[128,1024]{1,0:T(8,128)(2,1)}, u32[]{:S(2)}, u32[]{:S(2)}) collective-permute-start(bf16[128,1024]{1,0:T(8,128)(2,1)S(1)} %get-tuple-element.17), channel_id=1, source_target_pairs={} | collective-permute-start | bytes 786440 | tf_op jit(solution)/shard_map/ppermute | solution.py:16
  113.0 8.7 %collective-permute-start.14 = (bf16[128,1024]{1,0:T(8,128)(2,1)S(1)}, bf16[128,1024]{1,0:T(8,128)(2,1)}, u32[]{:S(2)}, u32[]{:S(2)}) collective-permute-start(bf16[128,1024]{1,0:T(8,128)(2,1)S(1)} %get-tuple-element.18), channel_id=1, source_target_pairs={{28,0},{29,1},{30,2},{31,3}} | collective-permute-start | bytes 786440 | tf_op jit(solution)/shard_map/ppermute | solution.py:16
  114.4 22.9 %collective-permute-start.13 = (bf16[128,1024]{1,0:T(8,128)(2,1)}, bf16[128,1024]{1,0:T(8,128)(2,1)}, u32[]{:S(2)}, u32[]{:S(2)}) collective-permute-start(bf16[128,1024]{1,0:T(8,128)(2,1)} %get-tuple-element.19), channel_id=1, source_target_pairs={{24,0},{28,4},{25,1},{29,5},{26,2},{30,6},{27,3},{31,7}} | collective-permute-start | bytes 786440 | tf_op jit(solution)/shard_map/ppermute | solution.py:16
  115.8 21.5 %collective-permute-start.12 = (bf16[128,1024]{1,0:T(8,128)(2,1)}, bf16[128,1024]{1,0:T(8,128)(2,1)}, u32[]{:S(2)}, u32[]{:S(2)}) collective-permute-start(bf16[128,1024]{1,0:T(8,128)(2,1)} %get-tuple-element.20), channel_id=1, source_target_pairs={{20,0},{24,4},{28,8},{21,1},{25,5},{29,9},{22,2},{26,6},{30,10},{2... | collective-permute-start | bytes 786440 | tf_op jit(solution)/shard_map/ppermute | solution.py:16
  119.2 20.1 %collective-permute-start.11 = (bf16[128,1024]{1,0:T(8,128)(2,1)}, bf16[128,1024]{1,0:T(8,128)(2,1)}, u32[]{:S(2)}, u32[]{:S(2)}) collective-permute-start(bf16[128,1024]{1,0:T(8,128)(2,1)} %get-tuple-element.21), channel_id=1, source_target_pairs={{16,0},{20,4},{24,8},{28,12},{17,1},{21,5},{25,9},{29,13},{18,2},{... | collective-permute-start | bytes 786440 | tf_op jit(solution)/shard_map/ppermute | solution.py:16
  120.4 37.2 %collective-permute-start.10 = (bf16[128,1024]{1,0:T(8,128)(2,1)}, bf16[128,1024]{1,0:T(8,128)(2,1)}, u32[]{:S(2)}, u32[]{:S(2)}) collective-permute-start(bf16[128,1024]{1,0:T(8,128)(2,1)} %get-tuple-element.22), channel_id=1, source_target_pairs={{12,0},{16,4},{20,8},{24,12},{28,16},{13,1},{17,5},{21,9},{25,13},... | collective-permute-start | bytes 786440 | tf_op jit(solution)/shard_map/ppermute | solution.py:16
  121.8 40.7 %collective-permute-start.9 = (bf16[128,1024]{1,0:T(8,128)(2,1)}, bf16[128,1024]{1,0:T(8,128)(2,1)}, u32[]{:S(2)}, u32[]{:S(2)}) collective-permute-start(bf16[128,1024]{1,0:T(8,128)(2,1)} %get-tuple-element.23), channel_id=1, source_target_pairs={{8,0},{12,4},{16,8},{20,12},{24,16},{28,20},{9,1},{13,5},{17,9},{2... | collective-permute-start | bytes 786440 | tf_op jit(solution)/shard_map/ppermute | solution.py:16
Sparse Core Ops, SparseCore 0:
  17.9 18.9 all-gather.1
  75.4 26.4 reduce-scatter.1
where the time goes:
time: 173 us; the launch traced here: 172 us
  waiting for transfers between devices  60.5 us (35%)
  matrix products  48.2 us (28%)
  starting transfers between devices  28.2 us (16%)
  between operations  14.4 us (8%)
  local copies, waits for them, and re-layouts  14.2 us (8%)
  other arithmetic  6.31 us (4%)
    ppermute x16, waiting for transfers between devices, passed_along(): lax.ppermute(value, axis, [(source, source + steps) for source in range(l...  60.5 us
    ppermute x16, starting transfers between devices, passed_along(): lax.ppermute(value, axis, [(source, source + steps) for source in range(l...  28.2 us
    dot_general x1, matrix products, local(): jnp.einsum('hofw,fhot->wht', score_gradient, query_four, preferred_elemen...  9.91 us
    dot_general x1, matrix products, local(): jnp.einsum('kgpn,nkd->pkgd', score_gradient, keys_all, preferred_element_...  9.34 us
    dot_general x1, matrix products, local(): lax.dot_general(lax.all_gather(cotangent, 'tp', axis=0, tiled=True), out_...  8.16 us
    dot_general x1, matrix products, local(): jnp.dot(attended, out_weight, preferred_element_type=jnp.float32)  6.88 us
    unnamed x17, local copies, waits for them, and re-layouts  5.05 us
    dot_general x1, matrix products, local(): jnp.einsum('hofw,fhot->wht', probabilities_narrow, grad_four, preferred_e...  4.87 us
  transfers between devices with their start and end apart: 18, of which 7 were waited for; matrix products, arithmetic and copies ran while one was open for 38% of the time, Pallas kernels for 0%

commit v1 on v0

--- a/solution.py
+++ b/solution.py
@@ -8,6 +8,7 @@
 KEY_VALUE_HEADS = 16
 HEAD_SIZE = 128
 WINDOW_SPAN = 1024
+LONGEST_SHARE = 4
 
 
 def passed_along(value, axis, steps):
@@ -34,12 +35,50 @@
     return unnorm / jnp.sum(unnorm, axis=-1, keepdims=True)
 
 
+def all_gather_tp(value, axis):
+    count = lax.axis_size(axis)
+    me = lax.axis_index(axis)
+    block = value[None]
+    step = count // 2
+    held = [value]
+    offsets = [0]
+    while step >= 1:
+        got = lax.ppermute(jnp.stack(held), axis, [(d, d ^ step) for d in range(count)])
+        held = held + [got[j] for j in range(len(held))]
+        offsets = offsets + [o ^ step for o in offsets]
+        step //= 2
+    stacked = jnp.stack(held)
+    inverse = [offsets.index(o) for o in range(count)]
+    by_offset = stacked[jnp.array(inverse)]
+    order = jnp.bitwise_xor(jnp.arange(count, dtype=jnp.int32), me)
+    ordered = by_offset[order]
+    return ordered.reshape((count * value.shape[0],) + value.shape[1:])
+
+
+def reduce_scatter_tp(value, axis):
+    count = lax.axis_size(axis)
+    me = lax.axis_index(axis)
+    rows = value.shape[0] // count
+    blocks = value.reshape((count, rows) + value.shape[1:])
+    order = jnp.bitwise_xor(jnp.arange(count, dtype=jnp.int32), me)
+    blocks = blocks[order]
+    step = 1
+    while step < count:
+        pairs = blocks.reshape((-1, 2) + blocks.shape[1:])
+        got = lax.ppermute(pairs[:, 1].astype(jnp.bfloat16), axis, [(d, d ^ step) for d in range(count)])
+        blocks = pairs[:, 0].astype(jnp.float32) + got.astype(jnp.float32)
+        step *= 2
+    return blocks[0].astype(jnp.bfloat16)
+
+
 def local(queries, encoded_key_rows, value_matrix_rows, out_weight, cotangent, doc_lengths):
     tok_rows = queries.shape[0]
     kv_cols = encoded_key_rows.shape[1]
     heads_kv = kv_cols // HEAD_SIZE
     query_group_size = QUERY_HEADS // KEY_VALUE_HEADS
-    reach_count = WINDOW_SPAN // tok_rows
+    tokens = tok_rows * lax.axis_size("ctx")
+    longest = tokens // LONGEST_SHARE
+    reach_count = -(-(min(WINDOW_SPAN, longest) - 1) // tok_rows)
     score_scale = (D / QUERY_HEADS) ** (-0.5)
     device = lax.axis_index("ctx")
     key_value = jnp.concatenate([encoded_key_rows, value_matrix_rows], axis=1)
@@ -65,14 +104,12 @@
         .astype(jnp.bfloat16)
         .reshape(tok_rows, heads_kv * query_group_size * HEAD_SIZE)
     )
-    layer_out = lax.psum_scatter(
+    layer_out = reduce_scatter_tp(
         jnp.dot(attended, out_weight, preferred_element_type=jnp.float32).astype(jnp.bfloat16),
         "tp",
-        scatter_dimension=0,
-        tiled=True,
     )
     attended_output_grad = lax.dot_general(
-        lax.all_gather(cotangent, "tp", axis=0, tiled=True),
+        all_gather_tp(cotangent, "tp"),
         out_weight,
         (((1,), (1,)), ((), ())),
         preferred_element_type=jnp.float32,

time: 173 us -> 72.7 us (0.42)
  the two profiles are of different devices: /device:TPU:11 before, /device:TPU:0 now
where the time goes in v1:
time: 72.7 us; the launch traced here: 72 us
  matrix products  25 us (34%)
  waiting for transfers between devices  15.6 us (21%)
  starting transfers between devices  14.6 us (20%)
  local copies, waits for them, and re-layouts  10.3 us (14%)
  other arithmetic  5.62 us (8%)
  between operations  0.95 us (1%)
    ppermute x4, waiting for transfers between devices, passed_along(): lax.ppermute(value, axis, [(source, source + steps) for source in range(l...  15.1 us
    ppermute x4, starting transfers between devices, passed_along(): lax.ppermute(value, axis, [(source, source + steps) for source in range(l...  11.1 us
    dot_general x1, matrix products, local(): lax.dot_general(all_gather_tp(cotangent, 'tp'), out_weight, (((1,), (1,))...  7.72 us
    dot_general x1, matrix products, local(): jnp.dot(attended, out_weight, preferred_element_type=jnp.float32)  5.8 us
    unnamed x19, local copies, waits for them, and re-layouts  4.08 us
    dot_general x1, matrix products, local(): jnp.einsum('kgpn,nkd->pkgd', score_gradient, keys_all, preferred_element_...  3.25 us
    dot_general x1, matrix products, local(): jnp.einsum('hofw,fhot->wht', score_gradient, query_four, preferred_elemen...  2.48 us
    ppermute x2, starting transfers between devices, all_gather_tp(): lax.ppermute(jnp.stack(held), axis, [(d, d ^ step) for d in range(count)])  1.93 us
  transfers between devices with their start and end apart: 8, of which 4 were waited for; matrix products, arithmetic and copies ran while one was open for 51% of the time, Pallas kernels for 0%

profile of v1, /device:TPU:0, one launch (start us, length us, event | category | flops | bytes accessed | tf_op | source)
XLA Modules:
  0.0 72.0 jit_solution(678355299085232750)
XLA Ops:
  0.6 1.0 %copy.43 = bf16[128,512]{0,1:T(8,128)(2,1)S(1)} copy(bf16[128,512]{1,0:T(8,128)(2,1)} %param.8) | data formatting | bytes 262144 | tf_op args[1]
  1.7 1.0 %copy.44 = bf16[128,512]{0,1:T(8,128)(2,1)S(1)} copy(bf16[128,512]{1,0:T(8,128)(2,1)} %param.9) | data formatting | bytes 262144 | tf_op args[2]
  2.7 4.9 %collective-permute-start.1 = (bf16[128,1024]{0,1:T(8,128)(2,1)S(1)}, bf16[128,1024]{0,1:T(8,128)(2,1)S(1)}, u32[]{:S(2)}, u32[]{:S(2)}) collective-permute-start(bf16[128,1024]{0,1:T(8,128)(2,1)S(1)} %pad_maximum_fusion.3), channel_id=1, source_target_pairs={{0,4},{4,8},{8,12},{12,16},{16,20},{20,24},{24,28},{1,5},{5,9},{9,... | collective-permute-start | bytes 786440 | tf_op jit(solution)/shard_map/ppermute | solution.py:17
  7.6 3.5 %collective-permute-start = (bf16[128,1024]{0,1:T(8,128)(2,1)S(1)}, bf16[128,1024]{0,1:T(8,128)(2,1)S(1)}, u32[]{:S(2)}, u32[]{:S(2)}) collective-permute-start(bf16[128,1024]{0,1:T(8,128)(2,1)S(1)} %pad_maximum_fusion.3), channel_id=1, source_target_pairs={{0,8},{4,12},{8,16},{12,20},{16,24},{20,28},{1,9},{5,13},{9,17},{1... | collective-permute-start | bytes 786440 | tf_op jit(solution)/shard_map/ppermute | solution.py:17
  11.1 1.6 %collective-permute-start.4 = (bf16[1,32,5376]{2,1,0:T(8,128)(2,1)}, bf16[1,32,5376]{2,1,0:T(8,128)(2,1)}, u32[]{:S(2)}, u32[]{:S(2)}) collective-permute-start(bf16[1,32,5376]{2,1,0:T(8,128)(2,1)} %bitcast.111), channel_id=1, source_target_pairs={{0,2},{1,3},{2,0},{3,1},{4,6},{5,7},{6,4},{7,5},{8,10},{9,11},{10,... | collective-permute-start | bytes 1032200 | tf_op jit(solution)/shard_map/ppermute | solution.py:46
  13.4 0.7 %copy.45 = s32[16,1]{1,0:T(8,128)S(1)} copy(s32[16,1]{0,1:T(1,128)} %bitcast.124) | data formatting | bytes 128 | tf_op jit(solution)/shard_map/reshape.152
  14.5 1.1 %copy.75 = bf16[128,1024]{0,1:T(8,128)(2,1)S(1)} copy(bf16[128,1024]{1,0:T(8,128)(2,1)} %param.7) | data formatting | bytes 524288 | tf_op jit(solution)/shard_map/reshape | solution.py:93
  16.6 1.8 %fusion.38 = (f32[4,2,128]{2,1,0:T(2,128)S(1)}, f32[4,2,128,384]{2,3,1,0:T(8,128)}) fusion(bf16[384,4,128,1]{0,2,3,1:T(8,128)(2,1)S(1)} %bitcast.119, bf16[128,4,2,128]{0,3,2,1:T(8,128)(2,1)S(1)} %bitcast.121, pred[128,384]{0,1:T(8,128)(4,1)S(1)} %fusion.26), kind=kOutput, calls=%fused_computation.71 | convolution fusion | flops 102236544 | bytes 2281472 | tf_op jit(solution)/shard_map/sub | solution.py:34
  18.4 1.7 %convolution_convert_fusion.2 = bf16[4,128,2,128]{3,1,2,0:T(8,128)(2,1)S(1)} fusion(bf16[384,4,128,1]{0,2,3,1:T(8,128)(2,1)S(1)} %bitcast.109, f32[4,2,128,384]{2,3,1,0:T(8,128)} %get-tuple-element.23, f32[4,2,128]{2,1,0:T(2,128)S(1)} %get-tuple-element.22), kind=kOutput, calls=%fused_computation.22 | convolution fusion | flops 101580800 | bytes 2232320 | tf_op jit(solution)/shard_map/kgpn,nkd->pkgd/dot_general | solution.py:101
  20.1 5.8 %convolution_convert_fusion = bf16[128,5376]{1,0:T(8,128)(2,1)S(1)} fusion(bf16[128,1024]{0,1:T(8,128)(2,1)S(1)} %bitcast.118, bf16[1024,5376]{1,0:T(8,128)(2,1)} %param.10), kind=kOutput, calls=%fused_computation.5 | convolution fusion | flops 1409974272 | bytes 12648448 | tf_op jit(solution)/shard_map/dot_general | solution.py:108
  26.9 1.0 %pad_maximum_fusion.2 = bf16[2,32,5376]{2,1,0:T(8,128)(2,1)S(1)} fusion(bf16[1,32,5376]{2,1,0:T(8,128)(2,1)} %collective-permute-done.4, bf16[1,32,5376]{2,1,0:T(8,128)(2,1)S(1)} %bitcast.112), kind=kLoop, calls=%fused_computation.36 | loop fusion | flops 344064 | bytes 1376256 | tf_op jit(solution)/shard_map/stack | solution.py:46
  29.0 0.8 %fusion.23 = bf16[1,32,5376]{2,1,0:T(8,128)(2,1)} fusion(f32[1,2,32,5376]{3,2,1,0:T(8,128)S(1)} %fusion.8), kind=kLoop, calls=%fused_computation.45 | loop fusion | bytes 688128 | tf_op jit(solution)/shard_map/convert_element_type | solution.py:68
  29.9 1.5 %collective-permute-start.3 = (bf16[1,32,5376]{2,1,0:T(8,128)(2,1)}, bf16[1,32,5376]{2,1,0:T(8,128)(2,1)}, u32[]{:S(2)}, u32[]{:S(2)}) collective-permute-start(bf16[1,32,5376]{2,1,0:T(8,128)(2,1)} %fusion.23), channel_id=1, source_target_pairs={{0,2},{1,3},{2,0},{3,1},{4,6},{5,7},{6,4},{7,5},{8,10},{9,11},{10,... | collective-permute-start | bytes 1032200 | tf_op jit(solution)/shard_map/ppermute | solution.py:68
  31.4 1.1 %pad_maximum_fusion.1 = bf16[4,32,5376]{2,1,0:T(8,128)(2,1)S(1)} fusion(bf16[2,32,5376]{2,1,0:T(8,128)(2,1)S(1)} %collective-permute-done.5, bf16[1,32,5376]{2,1,0:T(8,128)(2,1)} %collective-permute-done.4, bf16[1,32,5376]{2,1,0:T(8,128)(2,1)S(1)} %bitcast.113), kind=kLoop, calls=%fused_computation.18 | loop fusion | flops 1376256 | bytes 2752512 | tf_op jit(solution)/shard_map/stack | solution.py:50
  33.8 7.7 %convolution_convert_fusion.3 = bf16[128,1024]{1,0:T(8,128)(2,1)S(1)} fusion(bf16[128,5376]{1,0:T(8,128)(2,1)S(1)} %bitcast.105, bf16[1024,5376]{1,0:T(8,128)(2,1)} %param.10), kind=kOutput, calls=%fused_computation.23 | convolution fusion | flops 1409417216 | bytes 12648448 | tf_op jit(solution)/shard_map/dot_general | solution.py:111
  41.7 1.8 %fusion.19 = f32[4,128,384,1]{2,1,3,0:T(8,128)S(1)} fusion(bf16[128,4,2,128]{0,3,2,1:T(8,128)(2,1)S(1)} %bitcast.114, f32[4,2,128,384]{2,3,1,0:T(8,128)} %get-tuple-element.23, f32[4,2,128]{2,1,0:T(2,128)S(1)} %get-tuple-element.22), kind=kOutput, calls=%fused_computation.41 | convolution fusion | flops 101449728 | bytes 2625536 | tf_op jit(solution)/shard_map/hofw,fhot->wht/dot_general | solution.py:131
  44.4 3.2 %convolution_convert_fusion.1 = bf16[4,128,2,128]{3,1,2,0:T(8,128)(2,1)} fusion(bf16[384,4,128,1]{0,2,3,1:T(8,128)(2,1)S(1)} %bitcast.120, f32[4,384,128,2]{2,1,3,0:T(8,128)S(1)} %fusion.39, f32[4,2,128,384]{2,3,1,0:T(8,128)} %get-tuple-element.23, f32[4,2,128]{2,1,0:T(2,128)S(1)} %get-tuple-element.22), kind=kOutput, calls=%fused_computation.21 | convolution fusion | flops 103548288 | bytes 3805184 | tf_op jit(solution)/shard_map/kgpn,nkd->pkgd/dot_general | solution.py:124
  47.7 2.5 %fusion.9 = f32[4,384,128,1]{1,2,3,0:T(8,128)S(1)} fusion(bf16[128,4,2,128]{0,3,2,1:T(8,128)(2,1)S(1)} %bitcast.122, f32[4,384,128,2]{2,1,3,0:T(8,128)S(1)} %fusion.39, f32[4,2,128,384]{2,3,1,0:T(8,128)} %get-tuple-element.23, f32[4,2,128]{2,1,0:T(2,128)S(1)} %get-tuple-element.22), kind=kOutput, calls=%fused_computation.24 | convolution fusion | flops 103417216 | bytes 4198400 | tf_op jit(solution)/shard_map/hofw,fhot->wht/dot_general | solution.py:128
  51.1 0.8 %copy.59 = bf16[128,1024]{1,0:T(8,128)(2,1)} copy(bf16[128,1024]{0,1:T(8,128)(2,1)S(1)} %bitcast.123) | data formatting | bytes 524288
  52.1 1.4 %collective-permute-start.6 = (bf16[128,1024]{1,0:T(8,128)(2,1)S(1)}, bf16[128,1024]{1,0:T(8,128)(2,1)S(1)}, u32[]{:S(2)}, u32[]{:S(2)}) collective-permute-start(bf16[128,1024]{1,0:T(8,128)(2,1)S(1)} %get-tuple-element.16), channel_id=1, source_target_pairs={{4,0},{8,4},{12,8},{16,12},{20,16},{24,20},{28,24},{5,1},{9,5},{13... | collective-permute-start | bytes 786440 | tf_op jit(solution)/shard_map/ppermute | solution.py:17
  53.6 1.3 %collective-permute-start.7 = (bf16[128,1024]{1,0:T(8,128)(2,1)S(1)}, bf16[128,1024]{1,0:T(8,128)(2,1)S(1)}, u32[]{:S(2)}, u32[]{:S(2)}) collective-permute-start(bf16[128,1024]{1,0:T(8,128)(2,1)S(1)} %get-tuple-element.17), channel_id=1, source_target_pairs={{8,0},{12,4},{16,8},{20,12},{24,16},{28,20},{9,1},{13,5},{17,9},{2... | collective-permute-start | bytes 786440 | tf_op jit(solution)/shard_map/ppermute | solution.py:17
  54.9 1.8 %fusion.22 = bf16[32,5376]{1,0:T(8,128)(2,1)} fusion(bf16[1,32,5376]{2,1,0:T(8,128)(2,1)} %collective-permute-done.3, f32[1,2,32,5376]{3,2,1,0:T(8,128)S(1)} %copy-done.1), kind=kLoop, calls=%fused_computation.44 | loop fusion | flops 516096 | bytes 1376256 | tf_op jit(solution)/shard_map/convert_element_type | solution.py:71
  56.7 7.8 %collective-permute-done.6 = bf16[128,1024]{1,0:T(8,128)(2,1)S(1)} collective-permute-done((bf16[128,1024]{1,0:T(8,128)(2,1)S(1)}, bf16[128,1024]{1,0:T(8,128)(2,1)S(1)}, u32[]{:S(2)}, u32[]{:S(2)}) %collective-permute-start.6) | collective-permute-done | bytes 262176 | tf_op jit(solution)/shard_map/ppermute | solution.py:17
  64.4 6.8 %collective-permute-done.7 = bf16[128,1024]{1,0:T(8,128)(2,1)S(1)} collective-permute-done((bf16[128,1024]{1,0:T(8,128)(2,1)S(1)}, bf16[128,1024]{1,0:T(8,128)(2,1)S(1)}, u32[]{:S(2)}, u32[]{:S(2)}) %collective-permute-start.7) | collective-permute-done | bytes 262176 | tf_op jit(solution)/shard_map/ppermute | solution.py:17
  (51 shorter events, 8.3 us)
Async XLA Ops:
  2.7 13.1 %collective-permute-start.1 = (bf16[128,1024]{0,1:T(8,128)(2,1)S(1)}, bf16[128,1024]{0,1:T(8,128)(2,1)S(1)}, u32[]{:S(2)}, u32[]{:S(2)}) collective-permute-start(bf16[128,1024]{0,1:T(8,128)(2,1)S(1)} %pad_maximum_fusion.3), channel_id=1, source_target_pairs={{0,4},{4,8},{8,12},{12,16},{16,20},{20,24},{24,28},{1,5},{5,9},{9,... | collective-permute-start | bytes 786440 | tf_op jit(solution)/shard_map/ppermute | solution.py:17
  7.6 8.7 %collective-permute-start = (bf16[128,1024]{0,1:T(8,128)(2,1)S(1)}, bf16[128,1024]{0,1:T(8,128)(2,1)S(1)}, u32[]{:S(2)}, u32[]{:S(2)}) collective-permute-start(bf16[128,1024]{0,1:T(8,128)(2,1)S(1)} %pad_maximum_fusion.3), channel_id=1, source_target_pairs={{0,8},{4,12},{8,16},{12,20},{16,24},{20,28},{1,9},{5,13},{9,17},{1... | collective-permute-start | bytes 786440 | tf_op jit(solution)/shard_map/ppermute | solution.py:17
  11.1 15.6 %collective-permute-start.4 = (bf16[1,32,5376]{2,1,0:T(8,128)(2,1)}, bf16[1,32,5376]{2,1,0:T(8,128)(2,1)}, u32[]{:S(2)}, u32[]{:S(2)}) collective-permute-start(bf16[1,32,5376]{2,1,0:T(8,128)(2,1)} %bitcast.111), channel_id=1, source_target_pairs={{0,2},{1,3},{2,0},{3,1},{4,6},{5,7},{6,4},{7,5},{8,10},{9,11},{10,... | collective-permute-start | bytes 1032200 | tf_op jit(solution)/shard_map/ppermute | solution.py:46
  15.6 1.0 %copy-start.5 = (bf16[128,1024]{0,1:T(8,128)(2,1)}, bf16[128,1024]{0,1:T(8,128)(2,1)S(1)}, u32[]{:S(2)}) copy-start(bf16[128,1024]{0,1:T(8,128)(2,1)S(1)} %copy.75) | copy-start | bytes 786436
  16.6 1.8 %copy-start.3 = (bf16[384,512]{0,1:T(8,128)(2,1)}, bf16[384,512]{0,1:T(8,128)(2,1)S(1)}, u32[]{:S(2)}) copy-start(bf16[384,512]{0,1:T(8,128)(2,1)S(1)} %get-tuple-element.18) | copy-start | bytes 1179652
  25.9 1.0 %copy-start.2 = (bf16[32,5376]{1,0:T(8,128)(2,1)S(1)}, bf16[32,5376]{1,0:T(8,128)(2,1)}, u32[]{:S(2)}) copy-start(bf16[32,5376]{1,0:T(8,128)(2,1)} %param.11) | copy-start | bytes 1032196
  26.7 2.2 %collective-permute-start.2 = (bf16[2,32,5376]{2,1,0:T(8,128)(2,1)S(1)}, bf16[2,32,5376]{2,1,0:T(8,128)(2,1)S(1)}, u32[]{:S(2)}, u32[]{:S(2)}) collective-permute-start(bf16[2,32,5376]{2,1,0:T(8,128)(2,1)S(1)} %slice_bitcast_fusion.1), channel_id=1, source_target_pairs={{0,1},{1,0},{2,3},{3,2},{4,5},{5,4},{6,7},{7,6},{8,9},{9,8},{10,11... | collective-permute-start | bytes 2064392 | tf_op jit(solution)/shard_map/ppermute | solution.py:68
  28.0 3.4 %collective-permute-start.5 = (bf16[2,32,5376]{2,1,0:T(8,128)(2,1)S(1)}, bf16[2,32,5376]{2,1,0:T(8,128)(2,1)S(1)}, u32[]{:S(2)}, u32[]{:S(2)}) collective-permute-start(bf16[2,32,5376]{2,1,0:T(8,128)(2,1)S(1)} %pad_maximum_fusion.2), channel_id=1, source_target_pairs={{0,1},{1,0},{2,3},{3,2},{4,5},{5,4},{6,7},{7,6},{8,9},{9,8},{10,11... | collective-permute-start | bytes 2064392 | tf_op jit(solution)/shard_map/ppermute | solution.py:46
  29.0 2.3 %copy-start = (f32[1,2,32,5376]{3,2,1,0:T(8,128)}, f32[1,2,32,5376]{3,2,1,0:T(8,128)S(1)}, u32[]{:S(2)}) copy-start(f32[1,2,32,5376]{3,2,1,0:T(8,128)S(1)} %fusion.8) | copy-start | bytes 4128772
  29.9 25.0 %collective-permute-start.3 = (bf16[1,32,5376]{2,1,0:T(8,128)(2,1)}, bf16[1,32,5376]{2,1,0:T(8,128)(2,1)}, u32[]{:S(2)}, u32[]{:S(2)}) collective-permute-start(bf16[1,32,5376]{2,1,0:T(8,128)(2,1)} %fusion.23), channel_id=1, source_target_pairs={{0,2},{1,3},{2,0},{3,1},{4,6},{5,7},{6,4},{7,5},{8,10},{9,11},{10,... | collective-permute-start | bytes 1032200 | tf_op jit(solution)/shard_map/ppermute | solution.py:68
  43.4 1.0 %copy-start.4 = (bf16[384,512]{0,1:T(8,128)(2,1)S(1)}, bf16[384,512]{0,1:T(8,128)(2,1)}, u32[]{:S(2)}) copy-start(bf16[384,512]{0,1:T(8,128)(2,1)} %copy-done.3) | copy-start | bytes 1179652
  44.4 3.3 %copy-start.6 = (bf16[128,1024]{0,1:T(8,128)(2,1)S(1)}, bf16[128,1024]{0,1:T(8,128)(2,1)}, u32[]{:S(2)}) copy-start(bf16[128,1024]{0,1:T(8,128)(2,1)} %copy-done.5) | copy-start | bytes 786436
  50.2 1.0 %copy-start.7 = (bf16[4,128,2,128]{3,1,2,0:T(8,128)(2,1)S(1)}, bf16[4,128,2,128]{3,1,2,0:T(8,128)(2,1)}, u32[]{:S(2)}) copy-start(bf16[4,128,2,128]{3,1,2,0:T(8,128)(2,1)} %convolution_convert_fusion.1) | copy-start | bytes 786436
  52.0 2.9 %copy-start.1 = (f32[1,2,32,5376]{3,2,1,0:T(8,128)S(1)}, f32[1,2,32,5376]{3,2,1,0:T(8,128)}, u32[]{:S(2)}) copy-start(f32[1,2,32,5376]{3,2,1,0:T(8,128)} %copy-done) | copy-start | bytes 4128772
  52.1 12.3 %collective-permute-start.6 = (bf16[128,1024]{1,0:T(8,128)(2,1)S(1)}, bf16[128,1024]{1,0:T(8,128)(2,1)S(1)}, u32[]{:S(2)}, u32[]{:S(2)}) collective-permute-start(bf16[128,1024]{1,0:T(8,128)(2,1)S(1)} %get-tuple-element.16), channel_id=1, source_target_pairs={{4,0},{8,4},{12,8},{16,12},{20,16},{24,20},{28,24},{5,1},{9,5},{13... | collective-permute-start | bytes 786440 | tf_op jit(solution)/shard_map/ppermute | solution.py:17
  53.6 17.6 %collective-permute-start.7 = (bf16[128,1024]{1,0:T(8,128)(2,1)S(1)}, bf16[128,1024]{1,0:T(8,128)(2,1)S(1)}, u32[]{:S(2)}, u32[]{:S(2)}) collective-permute-start(bf16[128,1024]{1,0:T(8,128)(2,1)S(1)} %get-tuple-element.17), channel_id=1, source_target_pairs={{8,0},{12,4},{16,8},{20,12},{24,16},{28,20},{9,1},{13,5},{17,9},{2... | collective-permute-start | bytes 786440 | tf_op jit(solution)/shard_map/ppermute | solution.py:17

commit v2 on v0

v2 whole, which is shorter than its diff:
```python
import functools

import jax
import jax.numpy as jnp
from jax import lax
from jax.experimental import pallas as pl
from jax.experimental.pallas import tpu as pltpu
from jax.sharding import PartitionSpec as P

D = 5376
QUERY_HEADS = 32
KEY_VALUE_HEADS = 16
HEAD_SIZE = 128
WINDOW_SPAN = 1024
LONGEST_SHARE = 4

BF16 = jnp.bfloat16
F32 = jnp.float32
VMEM_LIMIT = 40 * 1024 * 1024


def passed_along(value, axis, steps):
    count = lax.axis_size(axis)
    leading, last = (max(0, -steps), min(count, count - steps))
    return lax.ppermute(value, axis, [(source, source + steps) for source in range(leading, last)])


def swapped(value, axis, step):
    return lax.ppermute(value, axis, [(d, d ^ step) for d in range(lax.axis_size(axis))])


def column_tile(width, most):
    return max(t for t in range(128, most + 1, 128) if width % t == 0)


def dot_nt(a, b):
    return lax.dot_general(a, b, (((1,), (1,)), ((), ())), preferred_element_type=F32)


def dot_nn(a, b):
    return lax.dot_general(a, b, (((1,), (0,)), ((), ())), preferred_element_type=F32)


def dot_tn(a, b):
    return lax.dot_general(a, b, (((0,), (0,)), ((), ())), preferred_element_type=F32)


def attended_grad_kernel(offsets, rows, me_ref, *refs):
    blocks, w_ref, out_ref, lhs_ref = refs[:-3], refs[-3], refs[-2], refs[-1]

    @pl.when(pl.program_id(0) == 0)
    def _():
        for slot, block in enumerate(blocks):
            lhs_ref[slot * rows : (slot + 1) * rows, :] = block[...]

    product = dot_nt(lhs_ref[...], w_ref[...]).astype(BF16)
    for slot, offset in enumerate(offsets):
        start = pl.multiple_of((me_ref[0] ^ offset) * rows, rows)
        out_ref[pl.ds(start, rows), :] = product[slot * rows : (slot + 1) * rows]


def attended_grad_of(blocks, offsets, out_weight, me):
    rows, width = blocks[0].shape
    heads_width = out_weight.shape[0]
    tokens = rows * len(blocks)
    tile = min(heads_width, 128)
    whole = pl.BlockSpec((rows, width), lambda i, *_: (0, 0))
    return pl.pallas_call(
        functools.partial(attended_grad_kernel, offsets, rows),
        out_shape=jax.ShapeDtypeStruct((tokens, heads_width), BF16),
        grid_spec=pltpu.PrefetchScalarGridSpec(
            num_scalar_prefetch=1,
            grid=(heads_width // tile,),
            in_specs=[whole] * len(blocks) + [pl.BlockSpec((tile, width), lambda i, *_: (i, 0))],
            out_specs=pl.BlockSpec((tokens, tile), lambda i, *_: (0, i)),
            scratch_shapes=[pltpu.VMEM((tokens, width), BF16)],
        ),
        compiler_params=pltpu.CompilerParams(vmem_limit_bytes=VMEM_LIMIT),
        cost_estimate=pl.CostEstimate(
            flops=2 * tokens * heads_width * width,
            bytes_accessed=2 * (heads_width * width + tokens * width + tokens * heads_width),
            transcendentals=0,
        ),
        name="attended_grad",
    )(me, *blocks, out_weight)


def attention_kernel(reach, kv_heads, group, scale, span, ctx_ref, lengths_ref, q_ref, g_ref, *refs):
    kv_refs = refs[: reach + 1]
    att_ref, dq_ref, own_ref = refs[reach + 1 : reach + 4]
    far_refs = refs[reach + 4 :]
    rows = q_ref.shape[0]
    width = kv_heads * HEAD_SIZE
    keys = (reach + 1) * rows
    first_query = ctx_ref[0] * rows
    query_pos = first_query + lax.broadcasted_iota(jnp.int32, (8, rows), 1)
    low = jnp.maximum(query_pos - (span - 1), 0)
    end = jnp.int32(0)
    for d in range(lengths_ref.shape[0]):
        end = end + lengths_ref[d]
        low = jnp.maximum(low, jnp.where(query_pos >= end, end, 0))
    low = low[:1]
    query_pos = query_pos[:1]
    key_pos = first_query - reach * rows + lax.broadcasted_iota(jnp.int32, (keys, rows), 0)
    allowed = (key_pos >= low) & (key_pos <= query_pos)
    bias = jnp.where(allowed, 0.0, -jnp.inf).astype(F32)
    bias = jnp.concatenate([bias] * group, axis=1)

    for head in range(kv_heads):
        columns = slice(head * HEAD_SIZE, (head + 1) * HEAD_SIZE)
        value_columns = slice(width + head * HEAD_SIZE, width + (head + 1) * HEAD_SIZE)
        k = jnp.concatenate([r[:, columns] for r in kv_refs], axis=0)
        v = jnp.concatenate([r[:, value_columns] for r in kv_refs], axis=0)
        group_columns = [
            slice((head * group + g) * HEAD_SIZE, (head * group + g + 1) * HEAD_SIZE) for g in range(group)
        ]
        q = jnp.concatenate([q_ref[:, c] for c in group_columns], axis=0)
        grad = jnp.concatenate([g_ref[:, c] for c in group_columns], axis=0)
        scores = dot_nt(k, q) * scale + bias
        unnorm = jnp.exp(scores - jnp.max(scores, axis=0, keepdims=True))
        probs = unnorm * (1.0 / jnp.sum(unnorm, axis=0, keepdims=True))
        probs_low = probs.astype(BF16)
        prob_grad = dot_nt(v, grad)
        delta = jnp.sum(probs * prob_grad, axis=0, keepdims=True)
        score_grad = (probs * (prob_grad - delta) * scale).astype(BF16)
        attended = dot_tn(probs_low, v).astype(BF16)
        query_grad = dot_tn(score_grad, k).astype(BF16)
        for g, c in enumerate(group_columns):
            att_ref[:, c] = attended[g * rows : (g + 1) * rows]
            dq_ref[:, c] = query_grad[g * rows : (g + 1) * rows]
        dk = dot_nn(score_grad, q)
        dv = dot_nn(probs_low, grad)
        for j, ref in enumerate(far_refs):
            ref[:, columns] = dk[j * rows : (j + 1) * rows].astype(ref.dtype)
            ref[:, value_columns] = dv[j * rows : (j + 1) * rows].astype(ref.dtype)
        own_ref[:, columns] = dk[reach * rows :]
        own_ref[:, value_columns] = dv[reach * rows :]


def attention_of(queries, grad, key_value_blocks, ctx, doc_lengths, scale, span):
    rows, q_width = queries.shape
    kv_width = key_value_blocks[0].shape[1]
    reach = len(key_value_blocks) - 1
    kv_heads = kv_width // (2 * HEAD_SIZE)
    group = q_width // (kv_heads * HEAD_SIZE)
    vmem = pl.BlockSpec(memory_space=pltpu.VMEM)
    smem = pl.BlockSpec(memory_space=pltpu.SMEM)
    keys = (reach + 1) * rows
    return pl.pallas_call(
        functools.partial(attention_kernel, reach, kv_heads, group, scale, span),
        out_shape=[
            jax.ShapeDtypeStruct((rows, q_width), BF16),
            jax.ShapeDtypeStruct((rows, q_width), BF16),
            jax.ShapeDtypeStruct((rows, kv_width), F32),
        ]
        + [jax.ShapeDtypeStruct((rows, kv_width), BF16)] * reach,
        in_specs=[smem, smem] + [vmem] * (reach + 3),
        out_specs=[vmem] * (reach + 3),
        compiler_params=pltpu.CompilerParams(vmem_limit_bytes=VMEM_LIMIT),
        cost_estimate=pl.CostEstimate(
            flops=12 * keys * rows * q_width,
            bytes_accessed=2 * (4 * rows * q_width + 2 * keys * kv_width),
            transcendentals=keys * rows * q_width // HEAD_SIZE,
        ),
        name="attention",
    )(ctx, doc_lengths, queries, grad, *key_value_blocks)


def projection_kernel(offsets, rows, me_ref, att_ref, w_ref, keep_ref, send_ref, lhs_ref):
    @pl.when(pl.program_id(0) == 0)
    def _():
        for slot, offset in enumerate(offsets):
            start = pl.multiple_of((me_ref[0] ^ offset) * rows, rows)
            lhs_ref[slot * rows : (slot + 1) * rows, :] = att_ref[pl.ds(start, rows), :]

    product = dot_nn(lhs_ref[...], w_ref[...])
    half = keep_ref.shape[0]
    keep_ref[...] = product[:half]
    send_ref[...] = product[half:].astype(send_ref.dtype)


def projection_of(attended, out_weight, me, offsets):
    tokens, heads_width = attended.shape
    width = out_weight.shape[1]
    rows = tokens // len(offsets)
    half = tokens // 2
    tile = column_tile(width, 1024)
    return pl.pallas_call(
        functools.partial(projection_kernel, offsets, rows),
        out_shape=[
            jax.ShapeDtypeStruct((half, width), F32),
            jax.ShapeDtypeStruct((half, width), BF16),
        ],
        grid_spec=pltpu.PrefetchScalarGridSpec(
            num_scalar_prefetch=1,
            grid=(width // tile,),
            in_specs=[
                pl.BlockSpec((tokens, heads_width), lambda i, *_: (0, 0)),
                pl.BlockSpec((heads_width, tile), lambda i, *_: (0, i)),
            ],
            out_specs=[
                pl.BlockSpec((half, tile), lambda i, *_: (0, i)),
                pl.BlockSpec((half, tile), lambda i, *_: (0, i)),
            ],
            scratch_shapes=[pltpu.VMEM((tokens, heads_width), BF16)],
        ),
        compiler_params=pltpu.CompilerParams(vmem_limit_bytes=VMEM_LIMIT),
        cost_estimate=pl.CostEstimate(
            flops=2 * tokens * heads_width * width,
            bytes_accessed=2 * (heads_width * width + 2 * tokens * width),
            transcendentals=0,
        ),
        name="projection",
    )(me, attended, out_weight)


def local(queries, encoded_key_rows, value_matrix_rows, out_weight, cotangent, doc_lengths):
    tok_rows = queries.shape[0]
    kv_cols = encoded_key_rows.shape[1]
    tokens = tok_rows * lax.axis_size("ctx")
    reach = -(-(min(WINDOW_SPAN, tokens // LONGEST_SHARE) - 1) // tok_rows)
    score_scale = (D / QUERY_HEADS) ** (-0.5)
    members = lax.axis_size("tp")
    rows = tok_rows // members
    me = lax.axis_index("tp").astype(jnp.int32).reshape(1)
    ctx = lax.axis_index("ctx").astype(jnp.int32).reshape(1)

    key_value = jnp.concatenate([encoded_key_rows, value_matrix_rows], axis=1)
    behind = [passed_along(key_value, "ctx", distance) for distance in range(reach, 0, -1)]

    blocks, offsets, step = [cotangent], [0], members // 2
    while step:
        blocks = blocks + [swapped(b, "tp", step) for b in blocks]
        offsets = offsets + [o ^ step for o in offsets]
        step //= 2
    grad = attended_grad_of(blocks, offsets, out_weight, me)

    attended, query_grad, own, *far = attention_of(
        queries, grad, behind + [key_value], ctx, doc_lengths, score_scale, WINDOW_SPAN
    )

    order = [j for j in range(members) if j % 2 == 0] + [j for j in range(members) if j % 2 == 1]
    keep, send = projection_of(attended, out_weight, me, order)
    held = [j for j in order if j % 2 == 0]
    step = 1
    while True:
        total = keep + swapped(send, "tp", step).astype(F32)
        step *= 2
        if step == members:
            break
        kept = [i for i, j in enumerate(held) if not j & step]
        sent = [i for i, j in enumerate(held) if j & step]
        keep = jnp.concatenate([total[i * rows : (i + 1) * rows] for i in kept], axis=0)
        send = jnp.concatenate([total[i * rows : (i + 1) * rows] for i in sent], axis=0).astype(BF16)
        held = [held[i] for i in kept]
    layer_out = total.astype(BF16)

    for distance, block in zip(range(reach, 0, -1), far):
        own = own + passed_along(block, "ctx", -distance).astype(F32)
    return (layer_out, query_grad, own[:, :kv_cols].astype(BF16), own[:, kv_cols:].astype(BF16))


def solution(mesh):
    in_specs = (
        P("ctx", "tp"),
        P("ctx", "tp"),
        P("ctx", "tp"),
        P("tp", None),
        P(("ctx", "tp"), None),
        P(),
    )
    out_specs = (P(("ctx", "tp"), None), P("ctx", "tp"), P("ctx", "tp"), P("ctx", "tp"))
    return jax.shard_map(local, mesh=mesh, in_specs=in_specs, out_specs=out_specs, check_vma=False)
```

time: 173 us -> 59 us (0.34)
  the two profiles are of different devices: /device:TPU:11 before, /device:TPU:4 now
where the time goes in v2:
time: 59 us; the launch traced here: 58.7 us
  waiting for transfers between devices  19.2 us (33%)
  starting transfers between devices  14.5 us (25%)
  Pallas kernels  12.5 us (21%)
  local copies, waits for them, and re-layouts  10.7 us (18%)
  other arithmetic  1.03 us (2%)
  between operations  0.75 us (1%)
    ppermute x4, starting transfers between devices, passed_along(): lax.ppermute(value, axis, [(source, source + steps) for source in range(l...  11.3 us
    ppermute x4, waiting for transfers between devices, passed_along(): lax.ppermute(value, axis, [(source, source + steps) for source in range(l...  10.7 us
    ppermute x5, waiting for transfers between devices, swapped(): lax.ppermute(value, axis, [(d, d ^ step) for d in range(lax.axis_size(axi...  8.53 us
    unnamed x15, local copies, waits for them, and re-layouts  8.38 us
    pallas_call x1, Pallas kernels, attended_grad_of(): pl.pallas_call(functools.partial(attended_grad_kernel, offsets, rows), ou...  4.4 us
    pallas_call x1, Pallas kernels, attention_of(): pl.pallas_call(functools.partial(attention_kernel, reach, kv_heads, group...  4.27 us
    pallas_call x1, Pallas kernels, projection_of(): pl.pallas_call(functools.partial(projection_kernel, offsets, rows), out_s...  3.8 us
    ppermute x5, starting transfers between devices, swapped(): lax.ppermute(value, axis, [(d, d ^ step) for d in range(lax.axis_size(axi...  3.19 us
  transfers between devices with their start and end apart: 9, of which 3 were waited for; matrix products, arithmetic and copies ran while one was open for 7% of the time, Pallas kernels for 8%

profile of v2, /device:TPU:4, one launch (start us, length us, event | category | flops | bytes accessed | tf_op | source)
XLA Modules:
  0.0 58.7 jit_solution(2052700420109750688)
XLA Ops:
  0.6 1.6 %collective-permute-start = (bf16[32,5376]{1,0:T(8,128)(2,1)}, bf16[32,5376]{1,0:T(8,128)(2,1)S(1)}, u32[]{:S(2)}, u32[]{:S(2)}) collective-permute-start(bf16[32,5376]{1,0:T(8,128)(2,1)} %refs_0_.1), channel_id=1, source_target_pairs={{0,2},{1,3},{2,0},{3,1},{4,6},{5,7},{6,4},{7,5},{8,10},{9,11},{10,... | collective-permute-start | bytes 1032200 | tf_op jit(solution)/shard_map/ppermute | solution.py:29
  2.2 8.5 %collective-permute-done.refs_1_ = bf16[32,5376]{1,0:T(8,128)(2,1)S(1)} collective-permute-done((bf16[32,5376]{1,0:T(8,128)(2,1)}, bf16[32,5376]{1,0:T(8,128)(2,1)S(1)}, u32[]{:S(2)}, u32[]{:S(2)}) %collective-permute-start) | collective-permute-done | bytes 344096 | tf_op jit(solution)/shard_map/ppermute | solution.py:29
  10.7 1.6 %constant_dynamic-update-slice_fusion.1 = bf16[128,1024]{1,0:T(8,128)(2,1)} fusion(bf16[128,512]{1,0:T(8,128)(2,1)} %param.7), kind=kLoop, calls=%fused_computation.6 | loop fusion | bytes 262144
  12.3 1.6 %constant_dynamic-update-slice_fusion.refs_2_ = bf16[128,1024]{1,0:T(8,128)(2,1)} fusion(bf16[128,1024]{1,0:T(8,128)(2,1)} %constant_dynamic-update-slice_fusion.1, bf16[128,512]{1,0:T(8,128)(2,1)} %param.8), kind=kLoop, calls=%fused_computation.5 | loop fusion | bytes 262144 | tf_op jit(solution)/shard_map/concatenate | solution.py:228
  13.8 3.4 %collective-permute-start.4 = (bf16[128,1024]{1,0:T(8,128)(2,1)}, bf16[128,1024]{1,0:T(8,128)(2,1)}, u32[]{:S(2)}, u32[]{:S(2)}) collective-permute-start(bf16[128,1024]{1,0:T(8,128)(2,1)} %constant_dynamic-update-slice_fusion.refs_2_), channel_id=1, source_target_pairs={{0,4},{4,8},{8,12},{12,16},{16,20},{20,24},{24,28},{1,5},{5,9},{9,... | collective-permute-start | bytes 786440 | tf_op jit(solution)/shard_map/ppermute | solution.py:25
  17.3 4.2 %collective-permute-start.3 = (bf16[128,1024]{1,0:T(8,128)(2,1)}, bf16[128,1024]{1,0:T(8,128)(2,1)}, u32[]{:S(2)}, u32[]{:S(2)}) collective-permute-start(bf16[128,1024]{1,0:T(8,128)(2,1)} %constant_dynamic-update-slice_fusion.refs_2_), channel_id=1, source_target_pairs={{0,8},{4,12},{8,16},{12,20},{16,24},{20,28},{1,9},{5,13},{9,17},{1... | collective-permute-start | bytes 786440 | tf_op jit(solution)/shard_map/ppermute | solution.py:25
  21.5 0.0 collective-permute-done.1.refs_2_
  21.5 0.7 %copy-done.3 = bf16[32,5376]{1,0:T(8,128)(2,1)} copy-done((bf16[32,5376]{1,0:T(8,128)(2,1)}, bf16[32,5376]{1,0:T(8,128)(2,1)S(1)}, u32[]{:S(2)}) %copy-start.3) | copy-done | bytes 344088
  22.2 4.1 %copy-done = bf16[1024,5376]{1,0:T(8,128)(2,1)S(1)} copy-done((bf16[1024,5376]{1,0:T(8,128)(2,1)S(1)}, bf16[1024,5376]{1,0:T(8,128)(2,1)}, u32[]{:S(2)}) %copy-start) | copy-done | bytes 11010072
  26.3 1.0 %copy-done.2 = bf16[32,5376]{1,0:T(8,128)(2,1)S(1)} copy-done((bf16[32,5376]{1,0:T(8,128)(2,1)S(1)}, bf16[32,5376]{1,0:T(8,128)(2,1)}, u32[]{:S(2)}) %copy-start.2) | copy-done | bytes 344088
  27.3 1.0 %copy-done.4 = bf16[32,5376]{1,0:T(8,128)(2,1)S(1)} copy-done((bf16[32,5376]{1,0:T(8,128)(2,1)S(1)}, bf16[32,5376]{1,0:T(8,128)(2,1)}, u32[]{:S(2)}) %copy-start.4) | copy-done | bytes 344088
  28.3 4.4 %attended_grad.1.g_ref = bf16[128,1024]{1,0:T(8,128)(2,1)S(1)} custom-call(s32[1]{0:T(128)} %bitcast.me_ref, bf16[32,5376]{1,0:T(8,128)(2,1)S(1)} %copy-done.2, bf16[32,5376]{1,0:T(8,128)(2,1)S(1)} %collective-permute-done.refs_1_, bf16[32,5376]{1,0:T(8,128)(2,1)S(1)} %collective-permute-done.1.refs_2_, bf16[32,5376]{1,0:T(8,128)(2,1)S(1)} %copy-done.4, ...), custom_call_target="tpu_custom_call" | custom-call | flops 1409286144 | bytes 12648448 | tf_op jit(solution)/shard_map/attended_grad/pallas_call | solution.py:68
  32.7 4.3 %attention.1 = (bf16[128,1024]{1,0:T(8,128)(2,1)S(1)}, bf16[128,1024]{1,0:T(8,128)(2,1)}, f32[128,1024]{1,0:T(8,128)S(1)}, bf16[128,1024]{1,0:T(8,128)(2,1)S(1)}, bf16[128,1024]{1,0:T(8,128)(2,1)S(1)}) custom-call(s32[1]{0:T(128)} %bitcast.1.ctx_ref, s32[16]{0:T(128)S(1)} %copy-done.6, bf16[128,1024]{1,0:T(8,128)(2,1)S(1)} %copy-done.5, ...), custom_call_target="tpu_custom_call" | custom-call | flops 603979776 | bytes 2621440 | tf_op jit(solution)/shard_map/attention/pallas_call | solution.py:149
  37.0 3.8 %projection.1 = (f32[64,5376]{1,0:T(8,128)S(1)}, bf16[64,5376]{1,0:T(8,128)(2,1)S(1)}) custom-call(s32[1]{0:T(128)} %bitcast.me_ref, bf16[128,1024]{1,0:T(8,128)(2,1)S(1)} %get-tuple-element.11.att_ref, bf16[1024,5376]{1,0:T(8,128)(2,1)S(1)} %copy-done.1), custom_call_target="tpu_custom_call" | custom-call | flops 1409286144 | bytes 13762560 | tf_op jit(solution)/shard_map/projection/pallas_call | solution.py:188
  40.8 0.1 collective-permute-start.5
  40.9 1.3 %collective-permute-start.7 = (bf16[128,1024]{1,0:T(8,128)(2,1)S(1)}, bf16[128,1024]{1,0:T(8,128)(2,1)S(1)}, u32[]{:S(2)}, u32[]{:S(2)}) collective-permute-start(bf16[128,1024]{1,0:T(8,128)(2,1)S(1)} %get-tuple-element.16), channel_id=1, source_target_pairs={{8,0},{12,4},{16,8},{20,12},{24,16},{28,20},{9,1},{13,5},{17,9},{2... | collective-permute-start | bytes 786440 | tf_op jit(solution)/shard_map/ppermute | solution.py:25
  42.2 2.4 %collective-permute-start.8 = (bf16[128,1024]{1,0:T(8,128)(2,1)S(1)}, bf16[128,1024]{1,0:T(8,128)(2,1)S(1)}, u32[]{:S(2)}, u32[]{:S(2)}) collective-permute-start(bf16[128,1024]{1,0:T(8,128)(2,1)S(1)} %get-tuple-element.17), channel_id=1, source_target_pairs={{4,0},{8,4},{12,8},{16,12},{20,16},{24,20},{28,24},{5,1},{9,5},{13... | collective-permute-start | bytes 786440 | tf_op jit(solution)/shard_map/ppermute | solution.py:25
  44.6 0.1 convert_add_fusion
  44.8 1.6 %collective-permute-start.6 = (bf16[32,5376]{1,0:T(8,128)(2,1)S(1)}, bf16[32,5376]{1,0:T(8,128)(2,1)S(1)}, u32[]{:S(2)}, u32[]{:S(2)}) collective-permute-start(bf16[32,5376]{1,0:T(8,128)(2,1)S(1)} %slice.27), channel_id=1, source_target_pairs={{0,2},{1,3},{2,0},{3,1},{4,6},{5,7},{6,4},{7,5},{8,10},{9,11},{10,... | collective-permute-start | bytes 1032200 | tf_op jit(solution)/shard_map/ppermute | solution.py:29
  46.4 5.1 %collective-permute-done.7 = bf16[128,1024]{1,0:T(8,128)(2,1)S(1)} collective-permute-done((bf16[128,1024]{1,0:T(8,128)(2,1)S(1)}, bf16[128,1024]{1,0:T(8,128)(2,1)S(1)}, u32[]{:S(2)}, u32[]{:S(2)}) %collective-permute-start.7) | collective-permute-done | bytes 262176 | tf_op jit(solution)/shard_map/ppermute | solution.py:25
  51.5 5.6 %collective-permute-done.8 = bf16[128,1024]{1,0:T(8,128)(2,1)S(1)} collective-permute-done((bf16[128,1024]{1,0:T(8,128)(2,1)S(1)}, bf16[128,1024]{1,0:T(8,128)(2,1)S(1)}, u32[]{:S(2)}, u32[]{:S(2)}) %collective-permute-start.8) | collective-permute-done | bytes 262176 | tf_op jit(solution)/shard_map/ppermute | solution.py:25
  57.0 0.1 add_convert_fusion
  57.2 0.7 %fusion.1 = (bf16[128,512]{1,0:T(8,128)(2,1)}, bf16[128,512]{1,0:T(8,128)(2,1)}) fusion(bf16[128,1024]{1,0:T(8,128)(2,1)S(1)} %add_convert_fusion), kind=kLoop, calls=%fused_computation.7 | loop fusion | bytes 524288 | tf_op jit(solution)/shard_map/slice | solution.py:260
  57.9 0.8 %fusion = bf16[32,5376]{1,0:T(8,128)(2,1)} fusion(f32[64,5376]{1,0:T(8,128)S(1)} %convert_add_fusion, bf16[32,5376]{1,0:T(8,128)(2,1)S(1)} %collective-permute-done.6), kind=kLoop, calls=%fused_computation.3 | loop fusion | flops 516096 | bytes 1376256 | tf_op jit(solution)/shard_map/convert_element_type | solution.py:256
  (18 shorter events, 0.1 us)
Async XLA Ops:
  0.6 10.1 %collective-permute-start = (bf16[32,5376]{1,0:T(8,128)(2,1)}, bf16[32,5376]{1,0:T(8,128)(2,1)S(1)}, u32[]{:S(2)}, u32[]{:S(2)}) collective-permute-start(bf16[32,5376]{1,0:T(8,128)(2,1)} %refs_0_.1), channel_id=1, source_target_pairs={{0,2},{1,3},{2,0},{3,1},{4,6},{5,7},{6,4},{7,5},{8,10},{9,11},{10,... | collective-permute-start | bytes 1032200 | tf_op jit(solution)/shard_map/ppermute | solution.py:29
  2.2 19.3 %collective-permute-start.1 = (bf16[32,5376]{1,0:T(8,128)(2,1)}, bf16[32,5376]{1,0:T(8,128)(2,1)S(1)}, u32[]{:S(2)}, u32[]{:S(2)}) collective-permute-start(bf16[32,5376]{1,0:T(8,128)(2,1)} %refs_0_.1), channel_id=1, source_target_pairs={{0,1},{1,0},{2,3},{3,2},{4,5},{5,4},{6,7},{7,6},{8,9},{9,8},{10,11... | collective-permute-start | bytes 1032200 | tf_op jit(solution)/shard_map/ppermute | solution.py:29
  10.7 10.8 %collective-permute-start.2 = (bf16[32,5376]{1,0:T(8,128)(2,1)S(1)}, bf16[32,5376]{1,0:T(8,128)(2,1)S(1)}, u32[]{:S(2)}, u32[]{:S(2)}) collective-permute-start(bf16[32,5376]{1,0:T(8,128)(2,1)S(1)} %collective-permute-done.refs_1_), channel_id=1, source_target_pairs={{0,1},{1,0},{2,3},{3,2},{4,5},{5,4},{6,7},{7,6},{8,9},{9,8},{10,11... | collective-permute-start | bytes 1032200 | tf_op jit(solution)/shard_map/ppermute | solution.py:29
  13.8 18.9 %collective-permute-start.4 = (bf16[128,1024]{1,0:T(8,128)(2,1)}, bf16[128,1024]{1,0:T(8,128)(2,1)}, u32[]{:S(2)}, u32[]{:S(2)}) collective-permute-start(bf16[128,1024]{1,0:T(8,128)(2,1)} %constant_dynamic-update-slice_fusion.refs_2_), channel_id=1, source_target_pairs={{0,4},{4,8},{8,12},{12,16},{16,20},{20,24},{24,28},{1,5},{5,9},{9,... | collective-permute-start | bytes 786440 | tf_op jit(solution)/shard_map/ppermute | solution.py:25
  17.3 15.5 %collective-permute-start.3 = (bf16[128,1024]{1,0:T(8,128)(2,1)}, bf16[128,1024]{1,0:T(8,128)(2,1)}, u32[]{:S(2)}, u32[]{:S(2)}) collective-permute-start(bf16[128,1024]{1,0:T(8,128)(2,1)} %constant_dynamic-update-slice_fusion.refs_2_), channel_id=1, source_target_pairs={{0,8},{4,12},{8,16},{12,20},{16,24},{20,28},{1,9},{5,13},{9,17},{1... | collective-permute-start | bytes 786440 | tf_op jit(solution)/shard_map/ppermute | solution.py:25
  21.5 0.7 %copy-start.3 = (bf16[32,5376]{1,0:T(8,128)(2,1)}, bf16[32,5376]{1,0:T(8,128)(2,1)S(1)}, u32[]{:S(2)}) copy-start(bf16[32,5376]{1,0:T(8,128)(2,1)S(1)} %collective-permute-done.2.refs_3_) | copy-start | bytes 1032196
  22.2 4.1 %copy-start = (bf16[1024,5376]{1,0:T(8,128)(2,1)S(1)}, bf16[1024,5376]{1,0:T(8,128)(2,1)}, u32[]{:S(2)}) copy-start(bf16[1024,5376]{1,0:T(8,128)(2,1)} %w_ref.1) | copy-start | bytes 33030148
  26.3 1.0 %copy-start.2 = (bf16[32,5376]{1,0:T(8,128)(2,1)S(1)}, bf16[32,5376]{1,0:T(8,128)(2,1)}, u32[]{:S(2)}) copy-start(bf16[32,5376]{1,0:T(8,128)(2,1)} %refs_0_.1) | copy-start | bytes 1032196
  27.3 1.0 %copy-start.4 = (bf16[32,5376]{1,0:T(8,128)(2,1)S(1)}, bf16[32,5376]{1,0:T(8,128)(2,1)}, u32[]{:S(2)}) copy-start(bf16[32,5376]{1,0:T(8,128)(2,1)} %copy-done.3) | copy-start | bytes 1032196
  28.3 4.4 %copy-start.5 = (bf16[128,1024]{1,0:T(8,128)(2,1)S(1)}, bf16[128,1024]{1,0:T(8,128)(2,1)}, u32[]{:S(2)}) copy-start(bf16[128,1024]{1,0:T(8,128)(2,1)} %q_ref.1) | copy-start | bytes 786436
  28.3 4.4 %copy-start.6 = (s32[16]{0:T(128)S(1)}, s32[16]{0:T(128)}, u32[]{:S(2)}) copy-start(s32[16]{0:T(128)} %lengths_ref.1) | copy-start | bytes 196
  28.3 8.7 %copy-start.1 = (bf16[1024,5376]{1,0:T(8,128)(2,1)S(1)}, bf16[1024,5376]{1,0:T(8,128)(2,1)}, u32[]{:S(2)}) copy-start(bf16[1024,5376]{1,0:T(8,128)(2,1)} %w_ref.1) | copy-start | bytes 33030148
  40.8 3.8 %collective-permute-start.5 = (bf16[64,5376]{1,0:T(8,128)(2,1)S(1)}, bf16[64,5376]{1,0:T(8,128)(2,1)S(1)}, u32[]{:S(2)}, u32[]{:S(2)}) collective-permute-start(bf16[64,5376]{1,0:T(8,128)(2,1)S(1)} %get-tuple-element.13), channel_id=1, source_target_pairs={{0,1},{1,0},{2,3},{3,2},{4,5},{5,4},{6,7},{7,6},{8,9},{9,8},{10,11... | collective-permute-start | bytes 2064392 | tf_op jit(solution)/shard_map/ppermute | solution.py:29
  40.9 10.6 %collective-permute-start.7 = (bf16[128,1024]{1,0:T(8,128)(2,1)S(1)}, bf16[128,1024]{1,0:T(8,128)(2,1)S(1)}, u32[]{:S(2)}, u32[]{:S(2)}) collective-permute-start(bf16[128,1024]{1,0:T(8,128)(2,1)S(1)} %get-tuple-element.16), channel_id=1, source_target_pairs={{8,0},{12,4},{16,8},{20,12},{24,16},{28,20},{9,1},{13,5},{17,9},{2... | collective-permute-start | bytes 786440 | tf_op jit(solution)/shard_map/ppermute | solution.py:25
  42.2 14.9 %collective-permute-start.8 = (bf16[128,1024]{1,0:T(8,128)(2,1)S(1)}, bf16[128,1024]{1,0:T(8,128)(2,1)S(1)}, u32[]{:S(2)}, u32[]{:S(2)}) collective-permute-start(bf16[128,1024]{1,0:T(8,128)(2,1)S(1)} %get-tuple-element.17), channel_id=1, source_target_pairs={{4,0},{8,4},{12,8},{16,12},{20,16},{24,20},{28,24},{5,1},{9,5},{13... | collective-permute-start | bytes 786440 | tf_op jit(solution)/shard_map/ppermute | solution.py:25
  44.8 13.0 %collective-permute-start.6 = (bf16[32,5376]{1,0:T(8,128)(2,1)S(1)}, bf16[32,5376]{1,0:T(8,128)(2,1)S(1)}, u32[]{:S(2)}, u32[]{:S(2)}) collective-permute-start(bf16[32,5376]{1,0:T(8,128)(2,1)S(1)} %slice.27), channel_id=1, source_target_pairs={{0,2},{1,3},{2,0},{3,1},{4,6},{5,7},{6,4},{7,5},{8,10},{9,11},{10,... | collective-permute-start | bytes 1032200 | tf_op jit(solution)/shard_map/ppermute | solution.py:29
